TPU v7x, 32 devices: a whole 2x2x4 slice. The times are simulated.
32 devices in a mesh: row: 4 (over y, x), query: 8 (over z, core).
Axes of the slice: x: 2, y: 2, z: 4, core: 2. Of those that a mesh axis runs over, the one named last changes fastest.
Arguments:
- logits: float32 [512, 1024], P('row'), may hold values from -9 to 309
- attributes: int32 [3, 16384], P(None, 'query'), may hold values from 0 to 63
- values: int32 [3, 16384], P(None, 'query'), may hold values from 0 to 15
- targets: float32 [16384], P('query'), may hold values from 0.25 to 1.75
Outputs:
- new_rows: float32 [512, 1024], P('row')
- residual: float32 [16384], P('query')
All inputs are finite; a program needn't handle non-finite values.
Results may differ from a plain program's by a relative error of at most 0.0064.
Values sent between devices are 32-bit elements; how exact they have to be, the bound alone decides.
A program may use at most 64 MiB of HBM per device.

v0:
```python
import jax
import jax.numpy as jnp
from jax import lax
from jax.sharding import PartitionSpec as P

VALS = 16
STEP_RATE = 2.0


def group_softmax(logit_rows):
    row_count = logit_rows.shape[0]
    grouped = logit_rows.reshape(row_count, -1, VALS)
    return jax.nn.softmax(grouped, axis=-1).reshape(row_count, -1)


def relaxed_update(logit_rows, relaxed, accumulated):
    row_count = logit_rows.shape[0]
    scaled = float(VALS * VALS) * accumulated
    grouped_p = relaxed.reshape(row_count, -1, VALS)
    grouped_d = scaled.reshape(row_count, -1, VALS)
    weighted_mean = jnp.sum(grouped_p * grouped_d, axis=-1, keepdims=True)
    tangent = (grouped_p * (grouped_d - weighted_mean)).reshape(row_count, -1)
    return group_softmax(logit_rows - STEP_RATE * tangent)


def make_selectors(columns, col_width):
    col_positions = jnp.arange(col_width, dtype=jnp.int32)[:, None]
    return [
        (col_positions == columns[slot_index][None, :]).astype(jnp.bfloat16)
        for slot_index in range(3)
    ]


def pick_columns(relaxed_b, selectors):
    return [
        jnp.dot(relaxed_b, selector, preferred_element_type=jnp.float32) for selector in selectors
    ]


def weight_sums(picked, misfit, selectors, running):
    weights = [
        (picked[1] * picked[2] * misfit).astype(jnp.bfloat16),
        (picked[0] * picked[2] * misfit).astype(jnp.bfloat16),
        (picked[0] * picked[1] * misfit).astype(jnp.bfloat16),
    ]
    for slot_index in range(3):
        running = running + lax.dot_general(
            weights[slot_index],
            selectors[slot_index],
            (((1,), (1,)), ((), ())),
            preferred_element_type=jnp.float32,
        )
    return running


def local(logits, attributes, values, targets):
    row_count, col_width = logits.shape
    total_rows = row_count * lax.axis_size("row")
    answer_scale = float(VALS**3) / total_rows
    relaxed = group_softmax(logits)
    relaxed_b = relaxed.astype(jnp.bfloat16)
    columns = attributes * VALS + values
    selectors = make_selectors(columns, col_width)
    picked = pick_columns(relaxed_b, selectors)
    partial_answers = jnp.sum(picked[0] * picked[1] * picked[2], axis=0)
    answers = lax.psum(partial_answers, "row") * answer_scale
    residual = answers - targets
    accumulated = weight_sums(
        picked, residual[None, :], selectors, jnp.zeros((row_count, col_width), jnp.float32)
    )
    share = lax.psum_scatter(accumulated, "query", scatter_dimension=1, tiled=True)
    share_width = share.shape[1]
    share_start = lax.axis_index("query") * share_width
    logit_share = lax.dynamic_slice_in_dim(logits, share_start, share_width, 1)
    relaxed_share = lax.dynamic_slice_in_dim(relaxed, share_start, share_width, 1)
    updated_share = relaxed_update(logit_share, relaxed_share, share)
    new_rows = lax.all_gather(updated_share, "query", axis=1, tiled=True)
    return (new_rows, residual)


def solution(mesh):
    placed = (P("row", None), P(None, "query"), P(None, "query"), P("query"))
    return jax.shard_map(
        local, mesh=mesh, in_specs=placed, out_specs=(P("row", None), P("query")), check_vma=False
    )
```

profile of v0, /device:TPU:0, one launch (start us, length us, event | category | flops | bytes accessed | tf_op | source)
XLA Modules:
  0.0 93.2 jit_solution(4023043113153630914)
XLA Ops:
  7.2 0.0 reduce-scatter.2.cloned.1.call-start
  7.2 1.2 %copy.6 = f32[128,1024]{0,1:T(8,128)S(1)} copy(f32[128,1024]{1,0:T(8,128)} %param.4) | data formatting | bytes 1048576 | tf_op args[0]
  8.4 0.1 bitcast_reduce_fusion
  8.5 1.5 %fusion.2 = f32[128,64,16]{0,2,1:T(8,128)S(1)} fusion(f32[128,1024]{0,1:T(8,128)S(1)} %copy.6, f32[128,64]{0,1:T(8,128)S(1)} %bitcast_reduce_fusion), kind=kOutput, calls=%fused_computation.2 | output fusion | flops 139279 | bytes 1081344 | tf_op jit(solution)/shard_map/div | solution.py:13
  10.0 0.2 copy.8
  10.2 0.0 copy-start.4
  10.3 0.2 copy.7
  10.5 0.5 copy-done.3
  11.0 0.0 copy-done.4
  11.1 0.3 copy-done
  11.3 0.2 exponential_divide_fusion
  11.5 1.8 %fusion.8 = f32[128,2048]{1,0:T(8,128)S(1)} fusion(s32[2048]{0:T(1024)S(1)} %bitcast.35, f32[128,1024]{1,0:T(8,128)S(1)} %exponential_divide_fusion), kind=kOutput, calls=%fused_computation.11 | convolution fusion | flops 539099136 | bytes 1581056 | tf_op jit(solution)/shard_map/dot_general | solution.py:36
  13.3 1.8 %fusion.4 = f32[128,2048]{1,0:T(8,128)S(1)} fusion(s32[2048]{0:T(1024)S(1)} %bitcast.37, f32[128,1024]{1,0:T(8,128)S(1)} %exponential_divide_fusion), kind=kOutput, calls=%fused_computation.5 | convolution fusion | flops 539099136 | bytes 1581056 | tf_op jit(solution)/shard_map/dot_general | solution.py:36
  15.1 2.8 %multiply_reduce_fusion = (f32[2048]{0:T(1024)S(1)}, f32[128,2048]{1,0:T(8,128)}, f32[128,2048]{1,0:T(8,128)S(1)}) fusion(f32[128,2048]{1,0:T(8,128)S(1)} %fusion.4, f32[128,2048]{1,0:T(8,128)S(1)} %fusion.8, s32[2048]{0:T(1024)S(1)} %bitcast.33, f32[128,1024]{1,0:T(8,128)S(1)} %exponential_divide_fusion), kind=kOutput, calls=%fused_computation.23 | convolution fusion | flops 539883520 | bytes 4734976 | tf_op jit(solution)/shard_map/dot_general | solution.py:36
  17.9 11.5 %psum.7 = f32[2048]{0:T(1024)S(1)} all-reduce(f32[2048]{0:T(1024)S(1)} %get-tuple-element.2), channel_id=1, replica_groups=mesh['row'=4,'query'=8] {'row'}, use_global_device_ids=true, to_apply=%region_3.0 | all-reduce | flops 2048 | bytes 16384 | tf_op jit(solution)/shard_map/psum | solution.py:66
  29.5 0.0 copy-start.6
  29.5 3.2 %fusion.3 = f32[128,1024]{1,0:T(8,128)S(1)} fusion(s32[2048]{0:T(1024)S(1)} %bitcast.38, f32[128,2048]{1,0:T(8,128)} %copy-done.1, f32[128,2048]{1,0:T(8,128)S(1)} %get-tuple-element.7, f32[2048]{0:T(1024)S(1)} %multiply_subtract_fusion.1), kind=kOutput, calls=%fused_computation.4 | convolution fusion | flops 539754496 | bytes 2637824 | tf_op jit(solution)/shard_map/dot_general | solution.py:47
  32.7 1.9 %fusion.5 = f32[128,1024]{1,0:T(8,128)S(1)} fusion(s32[2048]{0:T(1024)S(1)} %bitcast.34, f32[128,2048]{1,0:T(8,128)S(1)} %copy-done.2, f32[2048]{0:T(1024)S(1)} %multiply_subtract_fusion.1), kind=kOutput, calls=%fused_computation.7 | convolution fusion | flops 539492352 | bytes 1589248 | tf_op jit(solution)/shard_map/dot_general | solution.py:47
  34.6 2.7 %fusion.16 = f32[128,1024]{1,0:T(8,128)} fusion(f32[128,1024]{1,0:T(8,128)S(1)} %fusion.5, f32[128,1024]{1,0:T(8,128)S(1)} %fusion.3, s32[2048]{0:T(1024)S(1)} %bitcast.36, f32[128,2048]{1,0:T(8,128)S(1)} %fusion.4, f32[128,2048]{1,0:T(8,128)S(1)} %get-tuple-element.7, f32[2048]{0:T(1024)S(1)} %multiply_subtract_fusion.1), kind=kOutput, calls=%fused_computation.19 | convolution fusion | flops 540016640 | bytes 3686400 | tf_op jit(solution)/shard_map/dot_general | solution.py:47
  37.3 0.0 reduce-scatter.2.cloned.1.call-update
  37.4 30.5 %reduce-scatter.2.cloned.1.call-done = f32[128,128]{1,0:T(8,128)} async-done(((f32[128,1024]{1,0:T(8,128)}), f32[128,128]{1,0:T(8,128)}) %reduce-scatter.2.cloned.1.call-update) | async-done | bytes 65552 | tf_op jit(solution)/shard_map/reduce_scatter | solution.py:71
  67.9 0.9 multiply_multiply_fusion
  68.7 0.1 copy.9
  68.8 0.2 fusion.1
  69.0 0.1 copy.10
  69.1 0.9 multiply_subtract_fusion
  69.9 0.1 copy.11
  70.1 0.2 fusion
  70.3 0.1 copy.12
  70.4 0.1 copy.13
  70.5 15.0 %all_gather.3 = f32[128,1024]{1,0:T(8,128)S(1)} all-gather(f32[128,128]{1,0:T(8,128)S(1)} %exponential_divide_fusion.1), channel_id=1, replica_groups=mesh['row'=4,'query'=8] {'query'}, dimensions={1}, use_global_device_ids=true | all-gather | bytes 589824 | tf_op jit(solution)/shard_map/all_gather | solution.py:77
  85.5 0.8 copy.15
  (16 shorter events, 0.1 us)
Async XLA Ops:
  7.2 60.7 %reduce-scatter.2.cloned.1.call-start = ((), (), s32[]{:S(2)}) async-start(), calls=%async_computation.1 | async-start | bytes 589824 | tf_op jit(solution)/shard_map/reduce_scatter | solution.py:71
  10.2 0.8 copy-start.3
  10.2 0.8 copy-start.4
  10.3 1.1 %copy-start = (f32[128,1024]{1,0:T(8,128)S(1)}, f32[128,1024]{1,0:T(8,128)}, u32[]{:S(2)}) copy-start(f32[128,1024]{1,0:T(8,128)} %param.4) | copy-start | bytes 1572868
  13.3 1.8 %copy-start.1 = (f32[128,2048]{1,0:T(8,128)}, f32[128,2048]{1,0:T(8,128)S(1)}, u32[]{:S(2)}) copy-start(f32[128,2048]{1,0:T(8,128)S(1)} %fusion.8) | copy-start | bytes 3145732
  15.1 14.3 %copy-start.5 = (f32[2048]{0:T(1024)S(1)}, f32[2048]{0:T(1024)}, u32[]{:S(2)}) copy-start(f32[2048]{0:T(1024)} %param.7) | copy-start | bytes 24580
  29.5 5.1 %copy-start.6 = (f32[2048]{0:T(1024)}, f32[2048]{0:T(1024)S(1)}, u32[]{:S(2)}) copy-start(f32[2048]{0:T(1024)S(1)} %multiply_subtract_fusion.1) | copy-start | bytes 24580
  29.5 3.2 %copy-start.2 = (f32[128,2048]{1,0:T(8,128)S(1)}, f32[128,2048]{1,0:T(8,128)}, u32[]{:S(2)}) copy-start(f32[128,2048]{1,0:T(8,128)} %get-tuple-element.3) | copy-start | bytes 3145732
Sparse Core Ops, SparseCore 0:
  37.5 30.3 reduce-scatter.1
where the time goes:
time: 93.5 us; the launch traced here: 93.2 us
  waiting for transfers between devices  30.5 us (33%)
  blocking collectives  26.5 us (28%)
  between operations  14.3 us (15%)
  matrix products  14.2 us (15%)
  other arithmetic  3.85 us (4%)
  local copies, waits for them, and re-layouts  3.71 us (4%)
    reduce_scatter x1, waiting for transfers between devices, local(): lax.psum_scatter(accumulated, 'query', scatter_dimension=1, tiled=True)  30.5 us
    all_gather x1, blocking collectives, local(): new_rows = lax.all_gather(updated_share, 'query', axis=1, tiled=True)  15 us
    psum x1, blocking collectives, local(): answers = lax.psum(partial_answers, 'row') * answer_scale  11.5 us
    dot_general x3, matrix products, weight_sums(): lax.dot_general(weights[slot_index], selectors[slot_index], (((1,), (1,))...  7.81 us
    dot_general x3, matrix products, pick_columns(): jnp.dot(relaxed_b, selector, preferred_element_type=jnp.float32)  6.42 us
    unnamed x16, local copies, waits for them, and re-layouts  2.82 us
  transfers between devices with their start and end apart: 1, of which 1 were waited for; matrix products, arithmetic and copies ran while one was open for 0% of the time, Pallas kernels for 0%

commit v1 on v0

--- a/solution.py
+++ b/solution.py
@@ -5,6 +5,12 @@
 
 VALS = 16
 STEP_RATE = 2.0
+
+
+def laid_out(pieces, dim):
+    shape = list(pieces.shape[1:])
+    shape[dim] *= pieces.shape[0]
+    return jnp.moveaxis(pieces, 0, dim).reshape(shape)
 
 
 def group_softmax(logit_rows):
@@ -74,7 +80,19 @@
     logit_share = lax.dynamic_slice_in_dim(logits, share_start, share_width, 1)
     relaxed_share = lax.dynamic_slice_in_dim(relaxed, share_start, share_width, 1)
     updated_share = relaxed_update(logit_share, relaxed_share, share)
-    new_rows = lax.all_gather(updated_share, "query", axis=1, tiled=True)
+    size = lax.axis_size("query")
+    pairs = [(i, (i + 1) % size) for i in range(size)]
+    back = [(b, a) for a, b in pairs]
+    lower, upper = ([], [])
+    for step in range(size - 1):
+        if step % 2 == 0:
+            lower.append(lax.ppermute(lower[-1] if lower else updated_share, "query", pairs))
+        else:
+            upper.append(lax.ppermute(upper[-1] if upper else updated_share, "query", back))
+    tiles = jnp.stack([*lower[::-1], updated_share, *upper])
+    shift = lax.axis_index("query") - len(lower)
+    tiles = tiles[(jnp.arange(size) - shift) % size]
+    new_rows = laid_out(tiles, 1)
     return (new_rows, residual)
 
 

time: 93.5 us -> 102 us (1.091)
  blocking collectives: 26.5 us -> 11.5 us
  waiting for transfers between devices: 30.5 us -> 42 us
  starting transfers between devices: 0.04 us -> 10.8 us
  local copies, waits for them, and re-layouts: 3.71 us -> 4.75 us
    all_gather x1 -> x0, blocking collectives: 15 us -> none  [local(): new_rows = lax.all_gather(updated_share, 'query', axis=1, tiled=True)]
    ppermute x0 -> x7, waiting for transfers between devices: none -> 11.5 us  [the longest x4 11.4 us: local(): lax.ppermute(lower[-1] if lower else updated_share, 'query', pairs)]
    ppermute x0 -> x7, starting transfers between devices: none -> 10.8 us  [the longest x3 10.7 us: local(): lax.ppermute(upper[-1] if upper else updated_share, 'query', back)]
    unnamed x16 -> x23, local copies, waits for them, and re-layouts: 2.82 us -> 3.07 us
  transfers between devices with their start and end apart: 1 -> 8, of which waited for: 1 -> 5; matrix products, arithmetic and copies ran while one was open for 0% -> 0% of each run, Pallas kernels for 0% -> 0%
where the time goes in v1:
time: 102 us
  waiting for transfers between devices  42 us (41%)
  between operations  14.4 us (14%)
  matrix products  14.2 us (14%)
  blocking collectives  11.5 us (11%)
  starting transfers between devices  10.8 us (11%)
  local copies, waits for them, and re-layouts  4.75 us (5%)
  other arithmetic  3.87 us (4%)
    reduce_scatter x1, waiting for transfers between devices, local(): lax.psum_scatter(accumulated, 'query', scatter_dimension=1, tiled=True)  30.5 us
    psum x1, blocking collectives, local(): answers = lax.psum(partial_answers, 'row') * answer_scale  11.5 us
    ppermute x4, waiting for transfers between devices, local(): lax.ppermute(lower[-1] if lower else updated_share, 'query', pairs)  11.4 us
    ppermute x3, starting transfers between devices, local(): lax.ppermute(upper[-1] if upper else updated_share, 'query', back)  10.7 us
    dot_general x3, matrix products, weight_sums(): lax.dot_general(weights[slot_index], selectors[slot_index], (((1,), (1,))...  7.81 us
    dot_general x3, matrix products, pick_columns(): jnp.dot(relaxed_b, selector, preferred_element_type=jnp.float32)  6.42 us
    unnamed x23, local copies, waits for them, and re-layouts  3.07 us
  transfers between devices with their start and end apart: 8, of which 5 were waited for; matrix products, arithmetic and copies ran while one was open for 0% of the time, Pallas kernels for 0%

profile of v1, /device:TPU:0, one launch (start us, length us, event | category | flops | bytes accessed | tf_op | source)
XLA Modules:
  0.0 101.5 jit_solution(18396470967932403575)
XLA Ops:
  7.2 1.2 %copy.6 = f32[128,1024]{0,1:T(8,128)S(1)} copy(f32[128,1024]{1,0:T(8,128)} %param.4) | data formatting | bytes 1048576 | tf_op args[0]
  8.5 1.5 %fusion.2 = f32[128,64,16]{0,2,1:T(8,128)S(1)} fusion(f32[128,1024]{0,1:T(8,128)S(1)} %copy.6, f32[128,64]{0,1:T(8,128)S(1)} %bitcast_reduce_fusion), kind=kOutput, calls=%fused_computation.3 | output fusion | flops 139279 | bytes 1081344 | tf_op jit(solution)/shard_map/div | solution.py:19
  10.0 0.2 copy.8
  10.3 0.2 copy.7
  10.5 0.5 copy-done.3
  11.1 0.3 copy-done
  11.3 0.2 exponential_divide_fusion
  11.5 1.8 %fusion.8 = f32[128,2048]{1,0:T(8,128)S(1)} fusion(s32[2048]{0:T(1024)S(1)} %bitcast.57, f32[128,1024]{1,0:T(8,128)S(1)} %exponential_divide_fusion), kind=kOutput, calls=%fused_computation.12 | convolution fusion | flops 539099136 | bytes 1581056 | tf_op jit(solution)/shard_map/dot_general | solution.py:42
  13.3 1.8 %fusion.4 = f32[128,2048]{1,0:T(8,128)S(1)} fusion(s32[2048]{0:T(1024)S(1)} %bitcast.59, f32[128,1024]{1,0:T(8,128)S(1)} %exponential_divide_fusion), kind=kOutput, calls=%fused_computation.6 | convolution fusion | flops 539099136 | bytes 1581056 | tf_op jit(solution)/shard_map/dot_general | solution.py:42
  15.1 2.8 %multiply_reduce_fusion = (f32[2048]{0:T(1024)S(1)}, f32[128,2048]{1,0:T(8,128)}, f32[128,2048]{1,0:T(8,128)S(1)}) fusion(f32[128,2048]{1,0:T(8,128)S(1)} %fusion.4, f32[128,2048]{1,0:T(8,128)S(1)} %fusion.8, s32[2048]{0:T(1024)S(1)} %bitcast.55, f32[128,1024]{1,0:T(8,128)S(1)} %exponential_divide_fusion), kind=kOutput, calls=%fused_computation.24 | convolution fusion | flops 539883520 | bytes 4734976 | tf_op jit(solution)/shard_map/dot_general | solution.py:42
  17.9 11.5 %psum.7 = f32[2048]{0:T(1024)S(1)} all-reduce(f32[2048]{0:T(1024)S(1)} %get-tuple-element.4), channel_id=1, replica_groups=mesh['row'=4,'query'=8] {'row'}, use_global_device_ids=true, to_apply=%region_3.0 | all-reduce | flops 2048 | bytes 16384 | tf_op jit(solution)/shard_map/psum | solution.py:72
  29.5 3.2 %fusion.3 = f32[128,1024]{1,0:T(8,128)S(1)} fusion(s32[2048]{0:T(1024)S(1)} %bitcast.60, f32[128,2048]{1,0:T(8,128)} %copy-done.1, f32[128,2048]{1,0:T(8,128)S(1)} %get-tuple-element.9, f32[2048]{0:T(1024)S(1)} %multiply_subtract_fusion.1), kind=kOutput, calls=%fused_computation.5 | convolution fusion | flops 539754496 | bytes 2637824 | tf_op jit(solution)/shard_map/dot_general | solution.py:53
  32.7 1.9 %fusion.5 = f32[128,1024]{1,0:T(8,128)S(1)} fusion(s32[2048]{0:T(1024)S(1)} %bitcast.56, f32[128,2048]{1,0:T(8,128)S(1)} %copy-done.2, f32[2048]{0:T(1024)S(1)} %multiply_subtract_fusion.1), kind=kOutput, calls=%fused_computation.8 | convolution fusion | flops 539492352 | bytes 1589248 | tf_op jit(solution)/shard_map/dot_general | solution.py:53
  34.6 2.7 %fusion.16 = f32[128,1024]{1,0:T(8,128)} fusion(f32[128,1024]{1,0:T(8,128)S(1)} %fusion.5, f32[128,1024]{1,0:T(8,128)S(1)} %fusion.3, s32[2048]{0:T(1024)S(1)} %bitcast.58, f32[128,2048]{1,0:T(8,128)S(1)} %fusion.4, f32[128,2048]{1,0:T(8,128)S(1)} %get-tuple-element.9, f32[2048]{0:T(1024)S(1)} %multiply_subtract_fusion.1), kind=kOutput, calls=%fused_computation.20 | convolution fusion | flops 540016640 | bytes 3686400 | tf_op jit(solution)/shard_map/dot_general | solution.py:53
  37.4 30.5 %reduce-scatter.2.cloned.1.call-done = f32[128,128]{1,0:T(8,128)} async-done(((f32[128,1024]{1,0:T(8,128)}), f32[128,128]{1,0:T(8,128)}) %reduce-scatter.2.cloned.1.call-update) | async-done | bytes 65552 | tf_op jit(solution)/shard_map/reduce_scatter | solution.py:77
  67.9 0.9 multiply_multiply_fusion
  68.7 0.1 copy.9
  68.8 0.2 fusion.1
  69.0 0.1 copy.10
  69.1 0.9 multiply_subtract_fusion
  70.1 0.2 fusion
  70.4 0.1 copy.13
  70.6 5.5 %collective-permute-done = f32[128,128]{1,0:T(8,128)S(1)} collective-permute-done((f32[128,128]{1,0:T(8,128)S(1)}, f32[128,128]{1,0:T(8,128)S(1)}, u32[]{:S(2)}, u32[]{:S(2)}) %collective-permute-start) | collective-permute-done | bytes 65568 | tf_op jit(solution)/shard_map/ppermute | solution.py:89
  76.1 3.5 %collective-permute-start.4 = (f32[128,128]{1,0:T(8,128)S(1)}, f32[128,128]{1,0:T(8,128)S(1)}, u32[]{:S(2)}, u32[]{:S(2)}) collective-permute-start(f32[128,128]{1,0:T(8,128)S(1)} %exponential_divide_fusion.1), channel_id=1, source_target_pairs={{1,0},{2,1},{3,2},{4,3},{5,4},{6,5},{7,6},{0,7},{9,8},{10,9},{11,1... | collective-permute-start | bytes 196616 | tf_op jit(solution)/shard_map/ppermute | solution.py:91
  79.7 2.0 %collective-permute-done.1 = f32[128,128]{1,0:T(8,128)S(1)} collective-permute-done((f32[128,128]{1,0:T(8,128)S(1)}, f32[128,128]{1,0:T(8,128)S(1)}, u32[]{:S(2)}, u32[]{:S(2)}) %collective-permute-start.1) | collective-permute-done | bytes 65568 | tf_op jit(solution)/shard_map/ppermute | solution.py:89
  81.7 3.6 %collective-permute-start.5 = (f32[128,128]{1,0:T(8,128)S(1)}, f32[128,128]{1,0:T(8,128)S(1)}, u32[]{:S(2)}, u32[]{:S(2)}) collective-permute-start(f32[128,128]{1,0:T(8,128)S(1)} %collective-permute-done.4), channel_id=1, source_target_pairs={{1,0},{2,1},{3,2},{4,3},{5,4},{6,5},{7,6},{0,7},{9,8},{10,9},{11,1... | collective-permute-start | bytes 196616 | tf_op jit(solution)/shard_map/ppermute | solution.py:91
  85.3 2.0 %collective-permute-done.2 = f32[128,128]{1,0:T(8,128)S(1)} collective-permute-done((f32[128,128]{1,0:T(8,128)S(1)}, f32[128,128]{1,0:T(8,128)S(1)}, u32[]{:S(2)}, u32[]{:S(2)}) %collective-permute-start.2) | collective-permute-done | bytes 65568 | tf_op jit(solution)/shard_map/ppermute | solution.py:89
  87.3 3.6 %collective-permute-start.6 = (f32[128,128]{1,0:T(8,128)S(1)}, f32[128,128]{1,0:T(8,128)S(1)}, u32[]{:S(2)}, u32[]{:S(2)}) collective-permute-start(f32[128,128]{1,0:T(8,128)S(1)} %collective-permute-done.5), channel_id=1, source_target_pairs={{1,0},{2,1},{3,2},{4,3},{5,4},{6,5},{7,6},{0,7},{9,8},{10,9},{11,1... | collective-permute-start | bytes 196616 | tf_op jit(solution)/shard_map/ppermute | solution.py:91
  90.9 1.9 %collective-permute-done.3 = f32[128,128]{1,0:T(8,128)S(1)} collective-permute-done((f32[128,128]{1,0:T(8,128)S(1)}, f32[128,128]{1,0:T(8,128)S(1)}, u32[]{:S(2)}, u32[]{:S(2)}) %collective-permute-start.3) | collective-permute-done | bytes 65568 | tf_op jit(solution)/shard_map/ppermute | solution.py:89
  92.9 0.6 gather_fusion
  93.5 0.2 copy.14
  93.7 1.0 copy.15
  (41 shorter events, 0.6 us)
Async XLA Ops:
  7.2 60.7 %reduce-scatter.2.cloned.1.call-start = ((), (), s32[]{:S(2)}) async-start(), calls=%async_computation.1 | async-start | bytes 589824 | tf_op jit(solution)/shard_map/reduce_scatter | solution.py:77
  10.2 0.8 copy-start.3
  10.2 0.8 copy-start.4
  10.3 1.1 %copy-start = (f32[128,1024]{1,0:T(8,128)S(1)}, f32[128,1024]{1,0:T(8,128)}, u32[]{:S(2)}) copy-start(f32[128,1024]{1,0:T(8,128)} %param.4) | copy-start | bytes 1572868
  13.3 1.8 %copy-start.1 = (f32[128,2048]{1,0:T(8,128)}, f32[128,2048]{1,0:T(8,128)S(1)}, u32[]{:S(2)}) copy-start(f32[128,2048]{1,0:T(8,128)S(1)} %fusion.8) | copy-start | bytes 3145732
  15.1 14.3 %copy-start.5 = (f32[2048]{0:T(1024)S(1)}, f32[2048]{0:T(1024)}, u32[]{:S(2)}) copy-start(f32[2048]{0:T(1024)} %param.7) | copy-start | bytes 24580
  29.5 5.1 %copy-start.6 = (f32[2048]{0:T(1024)}, f32[2048]{0:T(1024)S(1)}, u32[]{:S(2)}) copy-start(f32[2048]{0:T(1024)S(1)} %multiply_subtract_fusion.1) | copy-start | bytes 24580
  29.5 3.2 %copy-start.2 = (f32[128,2048]{1,0:T(8,128)S(1)}, f32[128,2048]{1,0:T(8,128)}, u32[]{:S(2)}) copy-start(f32[128,2048]{1,0:T(8,128)} %get-tuple-element.5) | copy-start | bytes 3145732
  70.5 5.6 %collective-permute-start = (f32[128,128]{1,0:T(8,128)S(1)}, f32[128,128]{1,0:T(8,128)S(1)}, u32[]{:S(2)}, u32[]{:S(2)}) collective-permute-start(f32[128,128]{1,0:T(8,128)S(1)} %exponential_divide_fusion.1), channel_id=1, source_target_pairs={{0,1},{1,2},{2,3},{3,4},{4,5},{5,6},{6,7},{7,0},{8,9},{9,10},{10,1... | collective-permute-start | bytes 196616 | tf_op jit(solution)/shard_map/ppermute | solution.py:89
  76.1 5.6 %collective-permute-start.1 = (f32[128,128]{1,0:T(8,128)S(1)}, f32[128,128]{1,0:T(8,128)S(1)}, u32[]{:S(2)}, u32[]{:S(2)}) collective-permute-start(f32[128,128]{1,0:T(8,128)S(1)} %collective-permute-done), channel_id=1, source_target_pairs={{0,1},{1,2},{2,3},{3,4},{4,5},{5,6},{6,7},{7,0},{8,9},{9,10},{10,1... | collective-permute-start | bytes 196616 | tf_op jit(solution)/shard_map/ppermute | solution.py:89
  76.1 5.6 %collective-permute-start.4 = (f32[128,128]{1,0:T(8,128)S(1)}, f32[128,128]{1,0:T(8,128)S(1)}, u32[]{:S(2)}, u32[]{:S(2)}) collective-permute-start(f32[128,128]{1,0:T(8,128)S(1)} %exponential_divide_fusion.1), channel_id=1, source_target_pairs={{1,0},{2,1},{3,2},{4,3},{5,4},{6,5},{7,6},{0,7},{9,8},{10,9},{11,1... | collective-permute-start | bytes 196616 | tf_op jit(solution)/shard_map/ppermute | solution.py:91
  81.7 5.6 %collective-permute-start.2 = (f32[128,128]{1,0:T(8,128)S(1)}, f32[128,128]{1,0:T(8,128)S(1)}, u32[]{:S(2)}, u32[]{:S(2)}) collective-permute-start(f32[128,128]{1,0:T(8,128)S(1)} %collective-permute-done.1), channel_id=1, source_target_pairs={{0,1},{1,2},{2,3},{3,4},{4,5},{5,6},{6,7},{7,0},{8,9},{9,10},{10,1... | collective-permute-start | bytes 196616 | tf_op jit(solution)/shard_map/ppermute | solution.py:89
  81.7 5.6 %collective-permute-start.5 = (f32[128,128]{1,0:T(8,128)S(1)}, f32[128,128]{1,0:T(8,128)S(1)}, u32[]{:S(2)}, u32[]{:S(2)}) collective-permute-start(f32[128,128]{1,0:T(8,128)S(1)} %collective-permute-done.4), channel_id=1, source_target_pairs={{1,0},{2,1},{3,2},{4,3},{5,4},{6,5},{7,6},{0,7},{9,8},{10,9},{11,1... | collective-permute-start | bytes 196616 | tf_op jit(solution)/shard_map/ppermute | solution.py:91
  87.3 5.5 %collective-permute-start.3 = (f32[128,128]{1,0:T(8,128)S(1)}, f32[128,128]{1,0:T(8,128)S(1)}, u32[]{:S(2)}, u32[]{:S(2)}) collective-permute-start(f32[128,128]{1,0:T(8,128)S(1)} %collective-permute-done.2), channel_id=1, source_target_pairs={{0,1},{1,2},{2,3},{3,4},{4,5},{5,6},{6,7},{7,0},{8,9},{9,10},{10,1... | collective-permute-start | bytes 196616 | tf_op jit(solution)/shard_map/ppermute | solution.py:89
  87.3 5.6 %collective-permute-start.6 = (f32[128,128]{1,0:T(8,128)S(1)}, f32[128,128]{1,0:T(8,128)S(1)}, u32[]{:S(2)}, u32[]{:S(2)}) collective-permute-start(f32[128,128]{1,0:T(8,128)S(1)} %collective-permute-done.5), channel_id=1, source_target_pairs={{1,0},{2,1},{3,2},{4,3},{5,4},{6,5},{7,6},{0,7},{9,8},{10,9},{11,1... | collective-permute-start | bytes 196616 | tf_op jit(solution)/shard_map/ppermute | solution.py:91
Sparse Core Ops, SparseCore 0:
  37.5 30.3 reduce-scatter.1
